TPU v7x, 256 devices: a whole 4x4x8 slice. The times are simulated.
256 devices in a mesh: grp: 16 (over x_lo, z), blk: 16 (over x_hi, y, core).
Axes of the slice: x: 4 (x_hi: 2, x_lo: 2; x = x_hi * 2 + x_lo), y: 4, z: 8, core: 2. Of those that a mesh axis runs over, the one named last changes fastest.
Arguments:
- raw_ints: bfloat16 [2048, 256, 512], P('grp', 'blk'), may hold values from -0.59765625 to 0.59765625
- metric: bfloat16 [2048, 2048], P(None, 'grp'), as said below
- occ_energy: float32 [256], replicated, may hold values from -2 to -0.3
- virt_energy: float32 [512], replicated, may hold values from 0.2 to 5
Outputs:
- density: float32 [2048, 256, 512], P(None, ('blk', 'grp'))
- pair_energy: float32 [256, 4], P(('blk', 'grp'))
Inputs may be any that keep to these rules, and one draw needn't show every extreme that they name: `metric`: Symmetric.
All inputs are finite; a program needn't handle non-finite values.
Results may differ from a plain program's by a relative error of at most 0.0033.
Values may be sent and summed in bfloat16 or wider, within the bound.
A program may use at most 128 MiB of HBM per device.

v0:
```python
import jax
import jax.numpy as jnp
from jax import lax
from jax.sharding import PartitionSpec as P

VISITS = 4


def swapped(value, axis, bit):
    mask = 2**bit
    pairs = [(source, source ^ mask) for source in range(lax.axis_size(axis))]
    return lax.ppermute(value, axis, pairs)


def passed_along(block, axis, distance):
    devices = range(lax.axis_size(axis))
    route = [((i - distance) % len(devices), i) for i in devices]
    return lax.ppermute(block, axis, route)


def pair_terms(own, other, e_own, e_other, virt_energy):
    coulomb = lax.dot_general(
        own, other, (((0,), (0,)), ((), ())), preferred_element_type=jnp.float32
    )
    denom = e_own + e_other - virt_energy[:, None] - virt_energy[None, :]
    amplitude = coulomb / denom
    tilde = 2.0 * amplitude - amplitude.T
    energy = jnp.sum(coulomb * tilde)
    tilde_low = tilde.astype(jnp.bfloat16)
    contrib = lax.dot_general(
        other, tilde_low, (((1,), (1,)), ((), ())), preferred_element_type=jnp.float32
    )
    return (contrib, energy)


def local(raw_ints, metric, occ_energy, virt_energy):
    n_grp = lax.axis_size("grp")
    n_blk = lax.axis_size("blk")
    total_dev = n_grp * n_blk
    moved = lax.all_to_all(raw_ints, "grp", split_axis=1, concat_axis=0, tiled=True)
    own_raw = moved.reshape(moved.shape[0], moved.shape[2])
    own = jnp.dot(
        lax.all_gather(metric, "grp", axis=1, tiled=True),
        own_raw,
        preferred_element_type=jnp.float32,
    ).astype(jnp.bfloat16)
    place = lax.axis_index("grp") * n_blk + lax.axis_index("blk")

    def orbital_at(where_at):
        return where_at % n_blk * n_grp + where_at // n_blk

    e_own = lax.dynamic_index_in_dim(occ_energy, orbital_at(place), 0, keepdims=False)
    density, energy = pair_terms(own, own, e_own, e_own, virt_energy)
    energies = [energy]
    traveller = own
    for step in range(1, VISITS):
        partner = jnp.where(
            (place - step) % 2 == 0, (place - step) % total_dev, (place + step) % total_dev
        )
        if step % 2 == 1:
            traveller = swapped(traveller, ("grp", "blk"), 0)
        else:
            shifted = passed_along(traveller, ("grp", "blk"), 1)
            paired = swapped(shifted, ("grp", "blk"), 0)
            traveller = passed_along(paired, ("grp", "blk"), -1)
        e_other = lax.dynamic_index_in_dim(occ_energy, orbital_at(partner), 0, keepdims=False)
        contrib, energy = pair_terms(own, traveller, e_own, e_other, virt_energy)
        density = density + contrib
        energies.append(energy)
    return (density[:, None, :], jnp.stack(energies)[None, :])


def solution(mesh):
    in_specs = (P("grp", "blk", None), P(None, "grp"), P(), P())
    out_specs = (P(None, ("blk", "grp"), None), P(("blk", "grp"), None))
    return jax.shard_map(local, mesh=mesh, in_specs=in_specs, out_specs=out_specs, check_vma=False)
```

profile of v0, /device:TPU:1, one launch (start us, length us, event | category | flops | bytes accessed | tf_op | source)
XLA Modules:
  0.0 311.1 jit_solution(17193218113815496922)
XLA Ops:
  7.9 2.8 copy.11
  10.7 71.3 %all_to_all.15 = bf16[128,16,512]{2,0,1:T(8,128)(2,1)S(1)} all-to-all(bf16[128,16,512]{2,0,1:T(8,128)(2,1)S(1)} %copy.11), channel_id=1, replica_groups=mesh['grp'=16,'blk'=16] {'grp'}, dimensions={1} | all-to-all | bytes 4194304 | tf_op jit(solution)/shard_map/all_to_all | solution.py:40
  82.0 88.1 %all-gather.2.cloned.1.call-done = bf16[2048,2048]{1,0:T(8,128)(2,1)} async-done(((bf16[2048,128]{1,0:T(8,128)(2,1)}), bf16[2048,2048]{1,0:T(8,128)(2,1)}) %all-gather.2.cloned.1.call-update) | async-done | bytes 8388624 | tf_op jit(solution)/shard_map/all_gather | solution.py:43
  170.1 8.1 %convolution_convert_fusion = bf16[2048,512]{1,0:T(8,128)(2,1)S(1)} fusion(bf16[2048,2048]{1,0:T(8,128)(2,1)} %all-gather.2.cloned.1.call-done, bf16[2048,512]{1,0:T(8,128)(2,1)S(1)} %bitcast.67), kind=kOutput, calls=%fused_computation.1 | convolution fusion | flops 4296015872 | bytes 12582912 | tf_op jit(solution)/shard_map/dot_general | solution.py:42
  178.2 1.4 copy-done.9
  179.6 6.9 %collective-permute-start = (bf16[2048,512]{1,0:T(8,128)(2,1)S(1)}, bf16[2048,512]{1,0:T(8,128)(2,1)S(1)}, u32[]{:S(2)}, u32[]{:S(2)}) collective-permute-start(bf16[2048,512]{1,0:T(8,128)(2,1)S(1)} %convolution_convert_fusion), channel_id=1, source_target_pairs={{0,1},{1,0},{2,3},{3,2},{4,5},{5,4},{6,7},{7,6},{8,9},{9,8},{10,11... | collective-permute-start | bytes 6291464 | tf_op jit(solution)/shard_map/ppermute | solution.py:12
  186.5 3.8 %collective-permute-done = bf16[2048,512]{1,0:T(8,128)(2,1)S(1)} collective-permute-done((bf16[2048,512]{1,0:T(8,128)(2,1)S(1)}, bf16[2048,512]{1,0:T(8,128)(2,1)S(1)}, u32[]{:S(2)}, u32[]{:S(2)}) %collective-permute-start) | collective-permute-done | bytes 2097184 | tf_op jit(solution)/shard_map/ppermute | solution.py:12
  190.3 1.3 copy-done.13
  191.6 1.6 collective-permute-start.1
  193.1 23.0 %collective-permute-done.1 = bf16[2048,512]{1,0:T(8,128)(2,1)S(1)} collective-permute-done((bf16[2048,512]{1,0:T(8,128)(2,1)S(1)}, bf16[2048,512]{1,0:T(8,128)(2,1)S(1)}, u32[]{:S(2)}, u32[]{:S(2)}) %collective-permute-start.1) | collective-permute-done | bytes 2097184 | tf_op jit(solution)/shard_map/ppermute | solution.py:18
  216.1 6.7 %collective-permute-start.2 = (bf16[2048,512]{1,0:T(8,128)(2,1)S(1)}, bf16[2048,512]{1,0:T(8,128)(2,1)}, u32[]{:S(2)}, u32[]{:S(2)}) collective-permute-start(bf16[2048,512]{1,0:T(8,128)(2,1)S(1)} %collective-permute-done.1), channel_id=1, source_target_pairs={{0,1},{1,0},{2,3},{3,2},{4,5},{5,4},{6,7},{7,6},{8,9},{9,8},{10,11... | collective-permute-start | bytes 6291464 | tf_op jit(solution)/shard_map/ppermute | solution.py:12
  222.8 3.9 %collective-permute-done.2 = bf16[2048,512]{1,0:T(8,128)(2,1)} collective-permute-done((bf16[2048,512]{1,0:T(8,128)(2,1)S(1)}, bf16[2048,512]{1,0:T(8,128)(2,1)}, u32[]{:S(2)}, u32[]{:S(2)}) %collective-permute-start.2) | collective-permute-done | bytes 2097184 | tf_op jit(solution)/shard_map/ppermute | solution.py:12
  232.4 3.5 %fusion.16 = f32[512,512]{1,0:T(8,128)S(1)} fusion(bf16[2048,512]{1,0:T(8,128)(2,1)} %copy-done.9), kind=kOutput, calls=%fused_computation.27 | convolution fusion | flops 1073741824 | bytes 3145728 | tf_op jit(solution)/shard_map/dot_general | solution.py:22
  236.2 16.3 %collective-permute-done.3 = bf16[2048,512]{1,0:T(8,128)(2,1)} collective-permute-done((bf16[2048,512]{1,0:T(8,128)(2,1)}, bf16[2048,512]{1,0:T(8,128)(2,1)}, u32[]{:S(2)}, u32[]{:S(2)}) %collective-permute-start.3) | collective-permute-done | bytes 2097184 | tf_op jit(solution)/shard_map/ppermute | solution.py:18
  252.7 5.3 %fusion.9 = f32[2048,512]{1,0:T(8,128)} fusion(bf16[2048,512]{1,0:T(8,128)(2,1)} %copy-done.9, f32[512,512]{0,1:T(8,128)S(1)} %copy.12, f32[512,512]{1,0:T(8,128)S(1)} %fusion.16, f32[512]{0:T(512)S(1)} %copy-done.7, f32[512]{0:T(512)S(1)} %get-tuple-element.12), kind=kOutput, calls=%fused_computation.19 | convolution fusion | flops 1075576832 | bytes 8392704 | tf_op jit(solution)/shard_map/dot_general | solution.py:30
  259.7 5.6 %fusion.7 = f32[2048,512]{1,0:T(8,128)} fusion(bf16[2048,512]{1,0:T(8,128)(2,1)} %copy-done.13, f32[512,512]{0,1:T(8,128)S(1)} %copy.13, f32[512,512]{1,0:T(8,128)S(1)} %fusion.17, f32[512]{0:T(512)S(1)} %get-tuple-element.11, f32[512]{0:T(512)S(1)} %copy-done.7), kind=kOutput, calls=%fused_computation.17 | convolution fusion | flops 1075576832 | bytes 8392704 | tf_op jit(solution)/shard_map/dot_general | solution.py:30
  265.3 3.9 %fusion.18 = f32[512,512]{1,0:T(8,128)} fusion(bf16[2048,512]{1,0:T(8,128)(2,1)S(1)} %copy-done.11, bf16[2048,512]{1,0:T(8,128)(2,1)} %collective-permute-done.3), kind=kOutput, calls=%fused_computation.29 | convolution fusion | flops 1073741824 | bytes 5242880 | tf_op jit(solution)/shard_map/dot_general | solution.py:22
  269.2 1.6 copy.14
  270.9 5.6 %fusion.5 = f32[2048,512]{1,0:T(8,128)} fusion(bf16[2048,512]{1,0:T(8,128)(2,1)} %collective-permute-done.3, f32[512,512]{0,1:T(8,128)S(1)} %copy.14, f32[512,512]{1,0:T(8,128)S(1)} %copy-done.5, f32[512]{0:T(512)S(1)} %get-tuple-element.13, f32[512]{0:T(512)S(1)} %copy-done.7), kind=kOutput, calls=%fused_computation.15 | convolution fusion | flops 1075576832 | bytes 8392704 | tf_op jit(solution)/shard_map/dot_general | solution.py:30
  276.5 2.9 fusion.19
  279.7 4.4 %multiply_reduce_fusion.3 = (f32[]{:T(128)}, f32[]{:T(128)}, f32[]{:T(128)}, f32[]{:T(128)}) fusion(f32[512,512]{1,0:T(8,128)S(1)} %fusion.16, f32[512]{0:T(512)S(1)} %copy-done.7, f32[512]{0:T(512)S(1)} %get-tuple-element.12, f32[512,512]{0,1:T(8,128)} %copy-done.2, f32[512,512]{1,0:T(8,128)S(1)} %fusion.19, f32[512]{0:T(512)S(1)} %get-tuple-element.10, ...), kind=kLoop, calls=%fused_computation.13 | loop fusion | flops 8388604 | bytes 8398864 | tf_op jit(solution)/shard_map/reduce_sum | solution.py:28
  284.8 4.9 %add_bitcast_fusion = f32[2048,1,512]{2,0,1:T(8,128)S(1)} fusion(f32[2048,512]{1,0:T(8,128)} %fusion.5, f32[2048,512]{1,0:T(8,128)S(1)} %copy-done, f32[2048,512]{1,0:T(8,128)S(1)} %copy-done.1, bf16[2048,512]{1,0:T(8,128)(2,1)} %collective-permute-done.4, f32[512,512]{0,1:T(8,128)S(1)} %copy.15, f32[512,512]{1,0:T(8,128)S(1)} %fusion.19, ...), kind=kOutput, calls=%fused_computation | convolution fusion | flops 1078722560 | bytes 20975616 | tf_op jit(solution)/shard_map/dot_general | solution.py:30
  289.7 11.7 %copy.16 = f32[2048,1,512]{2,1,0:T(1,128)} copy(f32[2048,1,512]{2,0,1:T(8,128)S(1)} %add_bitcast_fusion) | data formatting | bytes 8388608
  301.4 2.9 maximum_bitcast_fusion
  (39 shorter events, 4.8 us)
Async XLA Ops:
  7.2 162.9 %all-gather.2.cloned.1.call-start = ((), (), s32[]{:S(2)}) async-start(), calls=%async_computation.1 | async-start | bytes 8912896 | tf_op jit(solution)/shard_map/all_gather | solution.py:43
  170.1 57.0 %copy-start.8 = (f32[256]{0:T(256)S(1)}, f32[256]{0:T(256)}, u32[]{:S(2)}) copy-start(f32[256]{0:T(256)} %param.6) | copy-start | bytes 3076
  170.1 62.3 %copy-start.7 = (f32[512]{0:T(512)S(1)}, f32[512]{0:T(512)}, u32[]{:S(2)}) copy-start(f32[512]{0:T(512)} %param.7) | copy-start | bytes 6148
  178.2 1.4 copy-start.9
  179.6 10.6 %collective-permute-start = (bf16[2048,512]{1,0:T(8,128)(2,1)S(1)}, bf16[2048,512]{1,0:T(8,128)(2,1)S(1)}, u32[]{:S(2)}, u32[]{:S(2)}) collective-permute-start(bf16[2048,512]{1,0:T(8,128)(2,1)S(1)} %convolution_convert_fusion), channel_id=1, source_target_pairs={{0,1},{1,0},{2,3},{3,2},{4,5},{5,4},{6,7},{7,6},{8,9},{9,8},{10,11... | collective-permute-start | bytes 6291464 | tf_op jit(solution)/shard_map/ppermute | solution.py:12
  190.3 1.3 copy-start.13
  191.6 24.5 %collective-permute-start.1 = (bf16[2048,512]{1,0:T(8,128)(2,1)S(1)}, bf16[2048,512]{1,0:T(8,128)(2,1)S(1)}, u32[]{:S(2)}, u32[]{:S(2)}) collective-permute-start(bf16[2048,512]{1,0:T(8,128)(2,1)S(1)} %collective-permute-done), channel_id=1, source_target_pairs={{255,0},{0,1},{1,2},{2,3},{3,4},{4,5},{5,6},{6,7},{7,8},{8,9},{9,1... | collective-permute-start | bytes 6291464 | tf_op jit(solution)/shard_map/ppermute | solution.py:18
  216.1 10.6 %collective-permute-start.2 = (bf16[2048,512]{1,0:T(8,128)(2,1)S(1)}, bf16[2048,512]{1,0:T(8,128)(2,1)}, u32[]{:S(2)}, u32[]{:S(2)}) collective-permute-start(bf16[2048,512]{1,0:T(8,128)(2,1)S(1)} %collective-permute-done.1), channel_id=1, source_target_pairs={{0,1},{1,0},{2,3},{3,2},{4,5},{5,4},{6,7},{7,6},{8,9},{9,8},{10,11... | collective-permute-start | bytes 6291464 | tf_op jit(solution)/shard_map/ppermute | solution.py:12
  226.8 25.8 %collective-permute-start.3 = (bf16[2048,512]{1,0:T(8,128)(2,1)}, bf16[2048,512]{1,0:T(8,128)(2,1)}, u32[]{:S(2)}, u32[]{:S(2)}) collective-permute-start(bf16[2048,512]{1,0:T(8,128)(2,1)} %collective-permute-done.2), channel_id=1, source_target_pairs={{1,0},{2,1},{3,2},{4,3},{5,4},{6,5},{7,6},{8,7},{9,8},{10,9},{11,1... | collective-permute-start | bytes 6291464 | tf_op jit(solution)/shard_map/ppermute | solution.py:18
  236.2 21.8 %copy-start.2 = (f32[512,512]{0,1:T(8,128)}, f32[512,512]{0,1:T(8,128)S(1)}, u32[]{:S(2)}) copy-start(f32[512,512]{0,1:T(8,128)S(1)} %copy.12) | copy-start | bytes 3145732
  252.5 24.0 %collective-permute-start.4 = (bf16[2048,512]{1,0:T(8,128)(2,1)}, bf16[2048,512]{1,0:T(8,128)(2,1)}, u32[]{:S(2)}, u32[]{:S(2)}) collective-permute-start(bf16[2048,512]{1,0:T(8,128)(2,1)} %collective-permute-done.3), channel_id=1, source_target_pairs={{0,1},{1,0},{2,3},{3,2},{4,5},{5,4},{6,7},{7,6},{8,9},{9,8},{10,11... | collective-permute-start | bytes 6291464 | tf_op jit(solution)/shard_map/ppermute | solution.py:12
  252.7 5.3 %copy-start.10 = (bf16[2048,512]{1,0:T(8,128)(2,1)S(1)}, bf16[2048,512]{1,0:T(8,128)(2,1)}, u32[]{:S(2)}) copy-start(bf16[2048,512]{1,0:T(8,128)(2,1)} %copy-done.9) | copy-start | bytes 6291460
  252.7 5.3 %copy-start.14 = (bf16[2048,512]{1,0:T(8,128)(2,1)S(1)}, bf16[2048,512]{1,0:T(8,128)(2,1)}, u32[]{:S(2)}) copy-start(bf16[2048,512]{1,0:T(8,128)(2,1)} %copy-done.13) | copy-start | bytes 6291460
  259.3 6.0 %copy-start.3 = (f32[512,512]{1,0:T(8,128)}, f32[512,512]{1,0:T(8,128)S(1)}, u32[]{:S(2)}) copy-start(f32[512,512]{1,0:T(8,128)S(1)} %fusion.17) | copy-start | bytes 3145732
  259.7 5.6 %copy-start.4 = (f32[512,512]{0,1:T(8,128)}, f32[512,512]{0,1:T(8,128)S(1)}, u32[]{:S(2)}) copy-start(f32[512,512]{0,1:T(8,128)S(1)} %copy.13) | copy-start | bytes 3145732
  259.7 5.6 %copy-start.11 = (bf16[2048,512]{1,0:T(8,128)(2,1)S(1)}, bf16[2048,512]{1,0:T(8,128)(2,1)}, u32[]{:S(2)}) copy-start(bf16[2048,512]{1,0:T(8,128)(2,1)} %copy-done.9) | copy-start | bytes 6291460
  269.2 1.7 copy-start.5
  270.8 5.7 %copy-start.6 = (f32[512,512]{0,1:T(8,128)}, f32[512,512]{0,1:T(8,128)S(1)}, u32[]{:S(2)}) copy-start(f32[512,512]{0,1:T(8,128)S(1)} %copy.14) | copy-start | bytes 3145732
  270.9 5.7 %copy-start.12 = (bf16[2048,512]{1,0:T(8,128)(2,1)S(1)}, bf16[2048,512]{1,0:T(8,128)(2,1)}, u32[]{:S(2)}) copy-start(bf16[2048,512]{1,0:T(8,128)(2,1)} %copy-done.9) | copy-start | bytes 6291460
  279.7 4.4 %copy-start = (f32[2048,512]{1,0:T(8,128)S(1)}, f32[2048,512]{1,0:T(8,128)}, u32[]{:S(2)}) copy-start(f32[2048,512]{1,0:T(8,128)} %fusion.9) | copy-start | bytes 12582916
  279.7 5.0 %copy-start.1 = (f32[2048,512]{1,0:T(8,128)S(1)}, f32[2048,512]{1,0:T(8,128)}, u32[]{:S(2)}) copy-start(f32[2048,512]{1,0:T(8,128)} %fusion.7) | copy-start | bytes 12582916
Sparse Core Ops, SparseCore 0:
  9.7 160.3 all-gather.1
where the time goes:
time: 312 us; the launch traced here: 311 us
  waiting for transfers between devices  136 us (44%)
  blocking collectives  71.3 us (23%)
  matrix products  41.1 us (13%)
  local copies, waits for them, and re-layouts  21 us (7%)
  between operations  18.8 us (6%)
  starting transfers between devices  15.8 us (5%)
  other arithmetic  7.37 us (2%)
    all_gather x1, waiting for transfers between devices, local(): lax.all_gather(metric, 'grp', axis=1, tiled=True)  88.1 us
    all_to_all x1, blocking collectives, local(): lax.all_to_all(raw_ints, 'grp', split_axis=1, concat_axis=0, tiled=True)  71.3 us
    ppermute x2, waiting for transfers between devices, passed_along(): return lax.ppermute(block, axis, route)  39.3 us
    dot_general x4, matrix products, pair_terms(): lax.dot_general(other, tilde_low, (((1,), (1,)), ((), ())), preferred_ele...  21.5 us
    unnamed x32, local copies, waits for them, and re-layouts  17.8 us
    ppermute x3, starting transfers between devices, swapped(): return lax.ppermute(value, axis, pairs)  13.8 us
    dot_general x4, matrix products, pair_terms(): lax.dot_general(own, other, (((0,), (0,)), ((), ())), preferred_element_t...  11.5 us
    dot_general x1, matrix products, local(): jnp.dot(lax.all_gather(metric, 'grp', axis=1, tiled=True), own_raw, prefe...  8.13 us
  transfers between devices with their start and end apart: 6, of which 5 were waited for; matrix products, arithmetic and copies ran while one was open for 10% of the time, Pallas kernels for 0%

commit v1 on v0

--- a/solution.py
+++ b/solution.py
@@ -40,7 +40,9 @@
     moved = lax.all_to_all(raw_ints, "grp", split_axis=1, concat_axis=0, tiled=True)
     own_raw = moved.reshape(moved.shape[0], moved.shape[2])
     own = jnp.dot(
-        lax.all_gather(metric, "grp", axis=1, tiled=True),
+        jnp.concatenate(
+            lax.all_to_all(jnp.stack([metric] * lax.axis_size("grp")), "grp", 0, 0), axis=1
+        ),
         own_raw,
         preferred_element_type=jnp.float32,
     ).astype(jnp.bfloat16)

time: 312 us -> 378 us (1.21)
  blocking collectives: 71.3 us -> 189 us
  waiting for transfers between devices: 136 us -> 94.4 us
  between operations: 18.8 us -> 5.46 us
  starting transfers between devices: 15.8 us -> 22 us
    all_to_all x1, blocking collectives: 71.3 us -> 189 us  [local(): lax.all_to_all(jnp.stack([metric] * lax.axis_size('grp')), 'grp', 0, 0)]
    all_gather x1 -> x0, waiting for transfers between devices: 88.1 us -> none  [local(): lax.all_gather(metric, 'grp', axis=1, tiled=True)]
    all_to_all x0 -> x1, waiting for transfers between devices: none -> 47.4 us  [local(): lax.all_to_all(raw_ints, 'grp', split_axis=1, concat_axis=0, tiled=True)]
    all_to_all x0 -> x1, starting transfers between devices: none -> 10.2 us  [local(): lax.all_to_all(raw_ints, 'grp', split_axis=1, concat_axis=0, tiled=True)]
    ppermute x3, starting transfers between devices: 13.8 us -> 9.88 us  [swapped(): return lax.ppermute(value, axis, pairs)]
    unnamed x32 -> x35, local copies, waits for them, and re-layouts: 17.8 us -> 18 us
  transfers between devices with their start and end apart: 6 -> 6, of which waited for: 5 -> 5; matrix products, arithmetic and copies ran while one was open for 10% -> 7% of each run, Pallas kernels for 0% -> 0%
where the time goes in v1:
time: 378 us
  blocking collectives  189 us (50%)
  waiting for transfers between devices  94.4 us (25%)
  matrix products  37.7 us (10%)
  local copies, waits for them, and re-layouts  22.3 us (6%)
  starting transfers between devices  22 us (6%)
  other arithmetic  7.37 us (2%)
  between operations  5.46 us (1%)
    all_to_all x1, blocking collectives, local(): lax.all_to_all(jnp.stack([metric] * lax.axis_size('grp')), 'grp', 0, 0)  189 us
    all_to_all x1, waiting for transfers between devices, local(): lax.all_to_all(raw_ints, 'grp', split_axis=1, concat_axis=0, tiled=True)  47.4 us
    ppermute x2, waiting for transfers between devices, passed_along(): return lax.ppermute(block, axis, route)  39.3 us
    dot_general x4, matrix products, pair_terms(): lax.dot_general(other, tilde_low, (((1,), (1,)), ((), ())), preferred_ele...  21.5 us
    unnamed x35, local copies, waits for them, and re-layouts  18 us
    dot_general x4, matrix products, pair_terms(): lax.dot_general(own, other, (((0,), (0,)), ((), ())), preferred_element_t...  11.5 us
    all_to_all x1, starting transfers between devices, local(): lax.all_to_all(raw_ints, 'grp', split_axis=1, concat_axis=0, tiled=True)  10.2 us
    ppermute x3, starting transfers between devices, swapped(): return lax.ppermute(value, axis, pairs)  9.88 us
  transfers between devices with their start and end apart: 6, of which 5 were waited for; matrix products, arithmetic and copies ran while one was open for 7% of the time, Pallas kernels for 0%

profile of v1, /device:TPU:1, one launch (start us, length us, event | category | flops | bytes accessed | tf_op | source)
XLA Modules:
  0.0 378.0 jit_solution(17965066926041343334)
XLA Ops:
  0.6 4.1 %copy.12 = bf16[128,16,512]{2,0,1:T(8,128)(2,1)} copy(bf16[128,16,512]{2,1,0:T(8,128)(2,1)} %param.4) | data formatting | bytes 4194304 | tf_op args[0]
  4.7 10.2 %all-to-all-start.1 = ((bf16[128,16,512]{2,0,1:T(8,128)(2,1)}), bf16[128,16,512]{2,0,1:T(8,128)(2,1)S(1)}, u32[]{:S(2)}, u32[]{:S(2)}) async-start(bf16[128,16,512]{2,0,1:T(8,128)(2,1)} %copy.12), calls=%async_computation.1 | async-start | bytes 4194304 | tf_op jit(solution)/shard_map/all_to_all | solution.py:40
  15.1 47.4 %all-to-all-done.1 = bf16[128,16,512]{2,0,1:T(8,128)(2,1)S(1)} async-done(((bf16[128,16,512]{2,0,1:T(8,128)(2,1)}), bf16[128,16,512]{2,0,1:T(8,128)(2,1)S(1)}, u32[]{:S(2)}, u32[]{:S(2)}) %all-to-all-start.1) | async-done | bytes 2097184 | tf_op jit(solution)/shard_map/all_to_all | solution.py:40
  63.6 188.7 %all_to_all.20 = bf16[16,2048,128]{1,2,0:T(8,128)(2,1)S(1)} all-to-all(bf16[16,2048,128]{1,2,0:T(8,128)(2,1)S(1)} %stack.12), channel_id=1, replica_groups=mesh['grp'=16,'blk'=16] {'grp'}, dimensions={0} | all-to-all | bytes 16777216 | tf_op jit(solution)/shard_map/all_to_all | solution.py:44
  252.3 4.8 %convolution_convert_fusion = bf16[2048,512]{1,0:T(8,128)(2,1)S(1)} fusion(bf16[2048,2048]{0,1:T(8,128)(2,1)S(1)} %bitcast.70, bf16[2048,512]{1,0:T(8,128)(2,1)S(1)} %bitcast.71), kind=kOutput, calls=%fused_computation.1 | convolution fusion | flops 4296015872 | bytes 12582912 | tf_op jit(solution)/shard_map/dot_general | solution.py:42
  257.1 1.4 copy-done.10
  258.5 3.2 collective-permute-start
  261.6 3.8 %collective-permute-done = bf16[2048,512]{1,0:T(8,128)(2,1)S(1)} collective-permute-done((bf16[2048,512]{1,0:T(8,128)(2,1)S(1)}, bf16[2048,512]{1,0:T(8,128)(2,1)S(1)}, u32[]{:S(2)}, u32[]{:S(2)}) %collective-permute-start) | collective-permute-done | bytes 2097184 | tf_op jit(solution)/shard_map/ppermute | solution.py:12
  265.4 1.6 collective-permute-start.1
  267.0 23.0 %collective-permute-done.1 = bf16[2048,512]{1,0:T(8,128)(2,1)S(1)} collective-permute-done((bf16[2048,512]{1,0:T(8,128)(2,1)S(1)}, bf16[2048,512]{1,0:T(8,128)(2,1)S(1)}, u32[]{:S(2)}, u32[]{:S(2)}) %collective-permute-start.1) | collective-permute-done | bytes 2097184 | tf_op jit(solution)/shard_map/ppermute | solution.py:18
  290.0 6.7 %collective-permute-start.2 = (bf16[2048,512]{1,0:T(8,128)(2,1)S(1)}, bf16[2048,512]{1,0:T(8,128)(2,1)}, u32[]{:S(2)}, u32[]{:S(2)}) collective-permute-start(bf16[2048,512]{1,0:T(8,128)(2,1)S(1)} %collective-permute-done.1), channel_id=1, source_target_pairs={{0,1},{1,0},{2,3},{3,2},{4,5},{5,4},{6,7},{7,6},{8,9},{9,8},{10,11... | collective-permute-start | bytes 6291464 | tf_op jit(solution)/shard_map/ppermute | solution.py:12
  296.7 3.9 %collective-permute-done.2 = bf16[2048,512]{1,0:T(8,128)(2,1)} collective-permute-done((bf16[2048,512]{1,0:T(8,128)(2,1)S(1)}, bf16[2048,512]{1,0:T(8,128)(2,1)}, u32[]{:S(2)}, u32[]{:S(2)}) %collective-permute-start.2) | collective-permute-done | bytes 2097184 | tf_op jit(solution)/shard_map/ppermute | solution.py:12
  306.2 3.5 fusion.16
  310.1 16.3 %collective-permute-done.3 = bf16[2048,512]{1,0:T(8,128)(2,1)} collective-permute-done((bf16[2048,512]{1,0:T(8,128)(2,1)}, bf16[2048,512]{1,0:T(8,128)(2,1)}, u32[]{:S(2)}, u32[]{:S(2)}) %collective-permute-start.3) | collective-permute-done | bytes 2097184 | tf_op jit(solution)/shard_map/ppermute | solution.py:18
  326.4 5.3 %fusion.9 = f32[2048,512]{1,0:T(8,128)} fusion(bf16[2048,512]{1,0:T(8,128)(2,1)} %copy-done.10, f32[512,512]{0,1:T(8,128)S(1)} %copy.13, f32[512,512]{1,0:T(8,128)S(1)} %fusion.16, f32[512]{0:T(512)S(1)} %copy-done.8, f32[512]{0:T(512)S(1)} %get-tuple-element.12), kind=kOutput, calls=%fused_computation.19 | convolution fusion | flops 1075576832 | bytes 8392704 | tf_op jit(solution)/shard_map/dot_general | solution.py:30
  333.4 5.6 %fusion.7 = f32[2048,512]{1,0:T(8,128)} fusion(bf16[2048,512]{1,0:T(8,128)(2,1)} %copy-done.14, f32[512,512]{0,1:T(8,128)S(1)} %copy.14, f32[512,512]{1,0:T(8,128)S(1)} %fusion.17, f32[512]{0:T(512)S(1)} %get-tuple-element.11, f32[512]{0:T(512)S(1)} %copy-done.8), kind=kOutput, calls=%fused_computation.17 | convolution fusion | flops 1075576832 | bytes 8392704 | tf_op jit(solution)/shard_map/dot_general | solution.py:30
  339.0 3.9 %fusion.18 = f32[512,512]{1,0:T(8,128)} fusion(bf16[2048,512]{1,0:T(8,128)(2,1)S(1)} %copy-done.12, bf16[2048,512]{1,0:T(8,128)(2,1)} %collective-permute-done.3), kind=kOutput, calls=%fused_computation.29 | convolution fusion | flops 1073741824 | bytes 5242880 | tf_op jit(solution)/shard_map/dot_general | solution.py:22
  342.8 1.6 copy.15
  344.5 5.6 %fusion.5 = f32[2048,512]{1,0:T(8,128)} fusion(bf16[2048,512]{1,0:T(8,128)(2,1)} %collective-permute-done.3, f32[512,512]{0,1:T(8,128)S(1)} %copy.15, f32[512,512]{1,0:T(8,128)S(1)} %copy-done.5, f32[512]{0:T(512)S(1)} %get-tuple-element.13, f32[512]{0:T(512)S(1)} %copy-done.8), kind=kOutput, calls=%fused_computation.15 | convolution fusion | flops 1075576832 | bytes 8392704 | tf_op jit(solution)/shard_map/dot_general | solution.py:30
  350.2 2.9 fusion.19
  353.4 4.4 %multiply_reduce_fusion.3 = (f32[]{:T(128)}, f32[]{:T(128)}, f32[]{:T(128)}, f32[]{:T(128)}) fusion(f32[512,512]{1,0:T(8,128)S(1)} %fusion.16, f32[512]{0:T(512)S(1)} %copy-done.8, f32[512]{0:T(512)S(1)} %get-tuple-element.12, f32[512,512]{0,1:T(8,128)} %copy-done.2, f32[512,512]{1,0:T(8,128)S(1)} %fusion.19, f32[512]{0:T(512)S(1)} %get-tuple-element.10, ...), kind=kLoop, calls=%fused_computation.13 | loop fusion | flops 8388604 | bytes 8398864 | tf_op jit(solution)/shard_map/reduce_sum | solution.py:28
  358.4 4.9 %add_bitcast_fusion = f32[2048,1,512]{2,0,1:T(8,128)S(1)} fusion(f32[2048,512]{1,0:T(8,128)} %fusion.5, f32[2048,512]{1,0:T(8,128)S(1)} %copy-done, f32[2048,512]{1,0:T(8,128)S(1)} %copy-done.1, bf16[2048,512]{1,0:T(8,128)(2,1)} %collective-permute-done.4, f32[512,512]{0,1:T(8,128)S(1)} %copy.16, f32[512,512]{1,0:T(8,128)S(1)} %fusion.19, ...), kind=kOutput, calls=%fused_computation | convolution fusion | flops 1078722560 | bytes 20975616 | tf_op jit(solution)/shard_map/dot_general | solution.py:30
  363.3 11.7 %copy.17 = f32[2048,1,512]{2,1,0:T(1,128)} copy(f32[2048,1,512]{2,0,1:T(8,128)S(1)} %add_bitcast_fusion) | data formatting | bytes 8388608
  375.0 2.9 maximum_bitcast_fusion
  (42 shorter events, 5.2 us)
Async XLA Ops:
  4.7 10.2 %copy-start.7 = (bf16[2048,128]{1,0:T(8,128)(2,1)S(1)}, bf16[2048,128]{1,0:T(8,128)(2,1)}, u32[]{:S(2)}) copy-start(bf16[2048,128]{1,0:T(8,128)(2,1)} %param.5) | copy-start | bytes 1572868
  4.7 57.8 %all-to-all-start.1 = ((bf16[128,16,512]{2,0,1:T(8,128)(2,1)}), bf16[128,16,512]{2,0,1:T(8,128)(2,1)S(1)}, u32[]{:S(2)}, u32[]{:S(2)}) async-start(bf16[128,16,512]{2,0,1:T(8,128)(2,1)} %copy.12), calls=%async_computation.1 | async-start | bytes 4194304 | tf_op jit(solution)/shard_map/all_to_all | solution.py:40
  252.3 48.7 %copy-start.9 = (f32[256]{0:T(256)S(1)}, f32[256]{0:T(256)}, u32[]{:S(2)}) copy-start(f32[256]{0:T(256)} %param.6) | copy-start | bytes 3076
  252.3 53.9 %copy-start.8 = (f32[512]{0:T(512)S(1)}, f32[512]{0:T(512)}, u32[]{:S(2)}) copy-start(f32[512]{0:T(512)} %param.7) | copy-start | bytes 6148
  257.1 1.4 copy-start.10
  258.5 6.9 %collective-permute-start = (bf16[2048,512]{1,0:T(8,128)(2,1)S(1)}, bf16[2048,512]{1,0:T(8,128)(2,1)S(1)}, u32[]{:S(2)}, u32[]{:S(2)}) collective-permute-start(bf16[2048,512]{1,0:T(8,128)(2,1)S(1)} %convolution_convert_fusion), channel_id=1, source_target_pairs={{0,1},{1,0},{2,3},{3,2},{4,5},{5,4},{6,7},{7,6},{8,9},{9,8},{10,11... | collective-permute-start | bytes 6291464 | tf_op jit(solution)/shard_map/ppermute | solution.py:12
  265.4 40.8 %copy-start.14 = (bf16[2048,512]{1,0:T(8,128)(2,1)}, bf16[2048,512]{1,0:T(8,128)(2,1)S(1)}, u32[]{:S(2)}) copy-start(bf16[2048,512]{1,0:T(8,128)(2,1)S(1)} %collective-permute-done) | copy-start | bytes 6291460
  265.4 24.5 %collective-permute-start.1 = (bf16[2048,512]{1,0:T(8,128)(2,1)S(1)}, bf16[2048,512]{1,0:T(8,128)(2,1)S(1)}, u32[]{:S(2)}, u32[]{:S(2)}) collective-permute-start(bf16[2048,512]{1,0:T(8,128)(2,1)S(1)} %collective-permute-done), channel_id=1, source_target_pairs={{255,0},{0,1},{1,2},{2,3},{3,4},{4,5},{5,6},{6,7},{7,8},{8,9},{9,1... | collective-permute-start | bytes 6291464 | tf_op jit(solution)/shard_map/ppermute | solution.py:18
  290.0 10.6 %collective-permute-start.2 = (bf16[2048,512]{1,0:T(8,128)(2,1)S(1)}, bf16[2048,512]{1,0:T(8,128)(2,1)}, u32[]{:S(2)}, u32[]{:S(2)}) collective-permute-start(bf16[2048,512]{1,0:T(8,128)(2,1)S(1)} %collective-permute-done.1), channel_id=1, source_target_pairs={{0,1},{1,0},{2,3},{3,2},{4,5},{5,4},{6,7},{7,6},{8,9},{9,8},{10,11... | collective-permute-start | bytes 6291464 | tf_op jit(solution)/shard_map/ppermute | solution.py:12
  300.6 25.8 %collective-permute-start.3 = (bf16[2048,512]{1,0:T(8,128)(2,1)}, bf16[2048,512]{1,0:T(8,128)(2,1)}, u32[]{:S(2)}, u32[]{:S(2)}) collective-permute-start(bf16[2048,512]{1,0:T(8,128)(2,1)} %collective-permute-done.2), channel_id=1, source_target_pairs={{1,0},{2,1},{3,2},{4,3},{5,4},{6,5},{7,6},{8,7},{9,8},{10,9},{11,1... | collective-permute-start | bytes 6291464 | tf_op jit(solution)/shard_map/ppermute | solution.py:18
  310.1 21.6 %copy-start.2 = (f32[512,512]{0,1:T(8,128)}, f32[512,512]{0,1:T(8,128)S(1)}, u32[]{:S(2)}) copy-start(f32[512,512]{0,1:T(8,128)S(1)} %copy.13) | copy-start | bytes 3145732
  326.4 23.8 %collective-permute-start.4 = (bf16[2048,512]{1,0:T(8,128)(2,1)}, bf16[2048,512]{1,0:T(8,128)(2,1)}, u32[]{:S(2)}, u32[]{:S(2)}) collective-permute-start(bf16[2048,512]{1,0:T(8,128)(2,1)} %collective-permute-done.3), channel_id=1, source_target_pairs={{0,1},{1,0},{2,3},{3,2},{4,5},{5,4},{6,7},{7,6},{8,9},{9,8},{10,11... | collective-permute-start | bytes 6291464 | tf_op jit(solution)/shard_map/ppermute | solution.py:12
  326.4 5.3 %copy-start.11 = (bf16[2048,512]{1,0:T(8,128)(2,1)S(1)}, bf16[2048,512]{1,0:T(8,128)(2,1)}, u32[]{:S(2)}) copy-start(bf16[2048,512]{1,0:T(8,128)(2,1)} %copy-done.10) | copy-start | bytes 6291460
  326.4 5.3 %copy-start.15 = (bf16[2048,512]{1,0:T(8,128)(2,1)S(1)}, bf16[2048,512]{1,0:T(8,128)(2,1)}, u32[]{:S(2)}) copy-start(bf16[2048,512]{1,0:T(8,128)(2,1)} %copy-done.14) | copy-start | bytes 6291460
  333.0 6.0 %copy-start.3 = (f32[512,512]{1,0:T(8,128)}, f32[512,512]{1,0:T(8,128)S(1)}, u32[]{:S(2)}) copy-start(f32[512,512]{1,0:T(8,128)S(1)} %fusion.17) | copy-start | bytes 3145732
  333.3 5.6 %copy-start.4 = (f32[512,512]{0,1:T(8,128)}, f32[512,512]{0,1:T(8,128)S(1)}, u32[]{:S(2)}) copy-start(f32[512,512]{0,1:T(8,128)S(1)} %copy.14) | copy-start | bytes 3145732
  333.4 5.6 %copy-start.12 = (bf16[2048,512]{1,0:T(8,128)(2,1)S(1)}, bf16[2048,512]{1,0:T(8,128)(2,1)}, u32[]{:S(2)}) copy-start(bf16[2048,512]{1,0:T(8,128)(2,1)} %copy-done.10) | copy-start | bytes 6291460
  342.8 1.7 copy-start.5
  344.5 5.7 %copy-start.6 = (f32[512,512]{0,1:T(8,128)}, f32[512,512]{0,1:T(8,128)S(1)}, u32[]{:S(2)}) copy-start(f32[512,512]{0,1:T(8,128)S(1)} %copy.15) | copy-start | bytes 3145732
  344.5 5.7 %copy-start.13 = (bf16[2048,512]{1,0:T(8,128)(2,1)S(1)}, bf16[2048,512]{1,0:T(8,128)(2,1)}, u32[]{:S(2)}) copy-start(bf16[2048,512]{1,0:T(8,128)(2,1)} %copy-done.10) | copy-start | bytes 6291460
  353.4 4.4 %copy-start = (f32[2048,512]{1,0:T(8,128)S(1)}, f32[2048,512]{1,0:T(8,128)}, u32[]{:S(2)}) copy-start(f32[2048,512]{1,0:T(8,128)} %fusion.9) | copy-start | bytes 12582916
  353.4 5.0 %copy-start.1 = (f32[2048,512]{1,0:T(8,128)S(1)}, f32[2048,512]{1,0:T(8,128)}, u32[]{:S(2)}) copy-start(f32[2048,512]{1,0:T(8,128)} %fusion.7) | copy-start | bytes 12582916
